TPU v7x, 32 devices: a whole 2x2x4 slice. The times are simulated.
32 devices in a mesh: dp: 16 (over z, y, x), seq: 2 (over core).
Axes of the slice: x: 2, y: 2, z: 4, core: 2. Of those that a mesh axis runs over, the one named last changes fastest.
Arguments:
- latents: float32 [16, 256, 48], P('dp', 'seq'), may hold values from -6 to 6
- valid: int32 [16, 256], P('dp', 'seq'), may hold values 0 or 1
- class_labels: int32 [16], replicated, may hold values from 0 to 447
- group_perm: int32 [16], P('dp'), may hold values from 0 to 15, as said below
- patch_weight: bfloat16 [48, 768], replicated, may hold values from -0.875 to 0.875
- pos_table: bfloat16 [256, 768], P('seq'), may hold values from -3 to 3
- class_table: bfloat16 [1024, 768], replicated, may hold values from -3 to 3
- ln1_gain: bfloat16 [1, 768], replicated, may hold values from 0.25 to 1.75
- ln1_bias: bfloat16 [1, 768], replicated, may hold values from -1.5 to 1.5
- qkv_weight: bfloat16 [1, 768, 2304], replicated, may hold values from -0.21875 to 0.21875
- out_weight: bfloat16 [1, 768, 768], replicated, may hold values from -0.875 to 0.875
- ln2_gain: bfloat16 [1, 768], replicated, may hold values from 0.25 to 1.75
- ln2_bias: bfloat16 [1, 768], replicated, may hold values from -1.5 to 1.5
- up_weight: bfloat16 [1, 768, 3072], replicated, may hold values from -0.21875 to 0.21875
- up_bias: bfloat16 [1, 3072], replicated, may hold values from -1.5 to 1.5
- down_weight: bfloat16 [1, 3072, 768], replicated, may hold values from -0.109375 to 0.109375
- head_weight: bfloat16 [768, 96], replicated, may hold values from -0.109375 to 0.109375
- head_bias: bfloat16 [96], replicated, may hold values from -1 to 1
- cot_latents: float32 [16, 256, 48], P('dp', 'seq'), may hold values from -6 to 6
- cot_logdet: float32 [16], P('dp'), may hold values from -4 to 4
Outputs:
- new_latents: float32 [16, 256, 48], P('dp', 'seq')
- logdet: float32 [16], P('dp')
- latents_grad: float32 [16, 256, 48], P('dp', 'seq')
- patch_weight_grad: float32 [48, 768], replicated
- pos_grad: float32 [256, 768], P('seq')
- class_grad: float32 [1024, 768], P('dp')
- ln1_gain_grad: float32 [1, 768], replicated
- ln1_bias_grad: float32 [1, 768], replicated
- qkv_grad: float32 [1, 768, 2304], replicated
- out_grad: float32 [1, 768, 768], replicated
- ln2_gain_grad: float32 [1, 768], replicated
- ln2_bias_grad: float32 [1, 768], replicated
- up_grad: float32 [1, 768, 3072], replicated
- up_bias_grad: float32 [1, 3072], replicated
- down_grad: float32 [1, 3072, 768], replicated
- head_weight_grad: float32 [768, 96], replicated
- head_bias_grad: float32 [96], replicated
Inputs may be any that keep to these rules, and one draw needn't show every extreme that they name: Each of 0 to 15 once; class_labels[group_perm] never falls.
All inputs are finite; a program needn't handle non-finite values. No bound on the sum of `valid` on one device may be relied on, other than what follows from the above.
Results may differ from a plain program's by a relative error of at most 0.023.
Values may be sent and summed in bfloat16 or wider, within the bound.
A program may use at most 320 MiB of HBM per device.

v0:
```python
import jax
import jax.numpy as jnp
from jax import lax
from jax.sharding import PartitionSpec as P

HEAD_DIM = 64
precise = lax.Precision.HIGHEST
norm_eps = 1e-05


def shifted_2(shard, axis, by):
    size = lax.axis_size(axis)
    pairs = [(i, i + by) for i in range(size) if 0 <= i + by < size]
    return lax.ppermute(shard, axis, pairs)


def layer_norm(values, norm_gain, norm_bias):
    center = values - jnp.mean(values, -1, keepdims=True)
    spread = jnp.mean(center * center, -1, keepdims=True)
    return center * lax.rsqrt(spread + norm_eps) * norm_gain + norm_bias


def matmul(left_side, weight_mat):
    return jnp.dot(left_side, weight_mat, preferred_element_type=jnp.float32)


def outer_sum(left_side, grad_side):
    left_flat = left_side.reshape(-1, left_side.shape[-1])
    grad_flat = grad_side.reshape(-1, grad_side.shape[-1])
    return lax.dot_general(
        left_flat, grad_flat, (((0,), (0,)), ((), ())), preferred_element_type=jnp.float32
    )


def transposed(grad_side, weight_mat):
    return lax.dot_general(
        grad_side,
        weight_mat,
        (((grad_side.ndim - 1,), (1,)), ((), ())),
        preferred_element_type=jnp.float32,
    )


def eight_rows(matrix):
    return matrix.reshape(8, -1)


def attention_mask(key_valid, patch_rows, seq_place):
    query_pos = seq_place * patch_rows + lax.iota(jnp.int32, patch_rows)
    key_pos = (seq_place - 1) * patch_rows + lax.iota(jnp.int32, 2 * patch_rows)
    earlier = (key_pos[None, :] < query_pos[:, None])[None] & (key_valid[:, None, :] > 0)
    return earlier | (key_pos[None, :] == query_pos[:, None])[None]


def masked_scores(query, keys, allowed):
    logits = jnp.einsum(
        "bqhd,bkhd->bhqk", query, keys, preferred_element_type=jnp.float32
    ) * HEAD_DIM ** (-0.5)
    return jnp.where(allowed[:, None], logits, -1e30)


def forward(latents, valid, class_rows, seq_place, weights):
    (
        patch_weight,
        pos_table,
        qkv_weight,
        out_weight,
        ln1_gain,
        ln1_bias,
        ln2_gain,
        ln2_bias,
        up_weight,
        up_bias,
        down_weight,
        head_weight,
        head_bias,
    ) = weights
    images, patch_rows, channels = latents.shape
    model_width = qkv_weight.shape[1]
    head_count = model_width // HEAD_DIM
    latent_low = latents.astype(jnp.bfloat16)
    hidden = (
        matmul(latent_low, patch_weight)
        + pos_table.astype(jnp.float32)[None]
        + class_rows[:, None, :]
    )
    own_mask = valid.astype(jnp.bfloat16)
    normed = layer_norm(
        hidden, ln1_gain[0].astype(jnp.float32), ln1_bias[0].astype(jnp.float32)
    ).astype(jnp.bfloat16)
    packed = matmul(normed, qkv_weight[0]).astype(jnp.bfloat16)
    query = packed[..., :model_width].reshape(images, patch_rows, head_count, HEAD_DIM)
    keys_own = packed[..., model_width : 2 * model_width]
    values_own = packed[..., 2 * model_width :]
    prior_keys, prior_values, prior_mask = shifted_2((keys_own, values_own, own_mask), "seq", 1)
    keys = jnp.concatenate((prior_keys, keys_own), 1).reshape(
        images, 2 * patch_rows, head_count, HEAD_DIM
    )
    values = jnp.concatenate((prior_values, values_own), 1).reshape(
        images, 2 * patch_rows, head_count, HEAD_DIM
    )
    allowed = attention_mask(jnp.concatenate((prior_mask, own_mask), 1), patch_rows, seq_place)
    logits = masked_scores(query, keys, allowed)
    row_peak = jnp.max(logits, -1, keepdims=True)
    log_total = row_peak + jnp.log(jnp.sum(jnp.exp(logits - row_peak), -1, keepdims=True))
    weights_soft = jnp.exp(logits - log_total).astype(jnp.bfloat16)
    attended = jnp.einsum(
        "bhqk,bkhd->bqhd", weights_soft, values, preferred_element_type=jnp.float32
    )
    attended = attended.astype(jnp.bfloat16).reshape(images, patch_rows, model_width)
    mid = hidden + matmul(attended, out_weight[0])
    second = layer_norm(
        mid, ln2_gain[0].astype(jnp.float32), ln2_bias[0].astype(jnp.float32)
    ).astype(jnp.bfloat16)
    preact = matmul(second, up_weight[0]) + up_bias[0].astype(jnp.float32)
    activated = jax.nn.gelu(preact, approximate=True).astype(jnp.bfloat16)
    saved = [
        (
            hidden,
            normed,
            query,
            keys,
            values,
            allowed,
            log_total,
            attended,
            mid,
            second,
            preact,
            activated,
        )
    ]
    hidden = mid + matmul(activated, down_weight[0])
    top_low = hidden.astype(jnp.bfloat16)
    head_out = matmul(top_low, head_weight) + head_bias.astype(jnp.float32)
    prior_row = shifted_2(head_out[:, patch_rows - 1, :], "seq", 1)
    shifted = jnp.concatenate((prior_row[:, None, :], head_out[:, : patch_rows - 1, :]), 1)
    shifted = shifted * valid.astype(jnp.float32)[..., None]
    alpha = shifted[..., :channels]
    shift_mean = shifted[..., channels:]
    factor = jnp.exp(-alpha)
    new_latents = (latents - shift_mean) * factor
    logdet_part = -jnp.sum(alpha, (1, 2))
    return (new_latents, logdet_part, factor, top_low, saved)


def local(
    latents,
    valid,
    class_labels,
    group_perm,
    patch_weight,
    pos_table,
    class_table,
    ln1_gain,
    ln1_bias,
    qkv_weight,
    out_weight,
    ln2_gain,
    ln2_bias,
    up_weight,
    up_bias,
    down_weight,
    head_weight,
    head_bias,
    cot_latents,
    cot_logdet,
):
    images, patch_rows, channels = latents.shape
    model_width = qkv_weight.shape[1]
    head_count = model_width // HEAD_DIM
    layer_total = qkv_weight.shape[0]
    seq_place = lax.axis_index("seq")
    picks = group_perm[:, None] == lax.iota(jnp.int32, class_labels.shape[0])[None, :]
    image_labels = jnp.sum(jnp.where(picks, class_labels[None, :], 0), 1)
    label_hot = image_labels[:, None] == lax.iota(jnp.int32, class_table.shape[0])[None, :]
    class_rows = matmul(label_hot.astype(jnp.bfloat16), class_table)
    weights = (
        patch_weight,
        pos_table,
        qkv_weight,
        out_weight,
        ln1_gain,
        ln1_bias,
        ln2_gain,
        ln2_bias,
        up_weight,
        up_bias,
        down_weight,
        head_weight,
        head_bias,
    )
    new_latents, logdet_part, factor, top_low, saved = forward(
        latents, valid, class_rows, seq_place, weights
    )
    latents_again, unused = lax.optimization_barrier((latents, new_latents))
    unused_a, unused_b, unused_c, unused_d, saved = forward(
        latents_again, valid, class_rows, seq_place, weights
    )
    valid_float = valid.astype(jnp.float32)
    d_alpha = -cot_latents * new_latents - cot_logdet[:, None, None]
    d_mean = -cot_latents * factor
    d_shifted = jnp.concatenate((d_alpha, d_mean), -1) * valid_float[..., None]
    next_row = shifted_2(d_shifted[:, 0, :], "seq", -1)
    d_head = jnp.concatenate((d_shifted[:, 1:, :], next_row[:, None, :]), 1).astype(jnp.bfloat16)
    head_weight_grad = outer_sum(top_low, d_head)
    head_bias_grad = jnp.sum(d_head.astype(jnp.float32), (0, 1))
    d_hidden = transposed(d_head, head_weight)
    grads_qkv, grads_out, grads_up, grads_down = ([], [], [], [])
    grads_g1, grads_b1, grads_g2, grads_b2, grads_ub = ([], [], [], [], [])
    for layer_index in reversed(range(layer_total)):
        (
            hidden,
            normed,
            query,
            keys,
            values,
            allowed,
            log_total,
            attended,
            mid,
            second,
            preact,
            activated,
        ) = saved[layer_index]
        d_down = d_hidden.astype(jnp.bfloat16)
        down_grad = outer_sum(activated, d_down)
        d_act = transposed(d_down, down_weight[layer_index])
        unused_gelu, gelu_pull = jax.vjp(lambda inner: jax.nn.gelu(inner, approximate=True), preact)
        d_pre = gelu_pull(d_act)[0].astype(jnp.bfloat16)
        up_bias_grad = jnp.sum(d_pre.astype(jnp.float32), (0, 1))
        up_grad = outer_sum(second, d_pre)
        d_second = transposed(d_pre, up_weight[layer_index])
        unused_norm, norm_pull = jax.vjp(
            layer_norm,
            mid,
            ln2_gain[layer_index].astype(jnp.float32),
            ln2_bias[layer_index].astype(jnp.float32),
        )
        d_mid_norm, ln2_gain_part, ln2_bias_part = norm_pull(d_second)
        d_mid = d_hidden + d_mid_norm
        d_proj = d_mid.astype(jnp.bfloat16)
        out_grad = outer_sum(attended, d_proj)
        d_attended = transposed(d_proj, out_weight[layer_index]).astype(jnp.bfloat16)
        d_attended = d_attended.reshape(images, patch_rows, head_count, HEAD_DIM)
        logits = masked_scores(query, keys, allowed)
        probs = jnp.exp(logits - log_total)
        d_probs = jnp.einsum(
            "bqhd,bkhd->bhqk", d_attended, values, preferred_element_type=jnp.float32
        )
        d_scores = (probs * (d_probs - jnp.sum(d_probs * probs, -1, keepdims=True))).astype(
            jnp.bfloat16
        )
        d_query = jnp.einsum(
            "bhqk,bkhd->bqhd", d_scores, keys, preferred_element_type=jnp.float32
        ) * HEAD_DIM ** (-0.5)
        d_keys = jnp.einsum(
            "bhqk,bqhd->bkhd", d_scores, query, preferred_element_type=jnp.float32
        ) * HEAD_DIM ** (-0.5)
        d_values = jnp.einsum(
            "bhqk,bqhd->bkhd",
            probs.astype(jnp.bfloat16),
            d_attended,
            preferred_element_type=jnp.float32,
        )
        d_keys = d_keys.reshape(images, 2 * patch_rows, model_width)
        d_values = d_values.reshape(images, 2 * patch_rows, model_width)
        back_keys, back_values = (
            shifted_2(d_keys[:, :patch_rows].astype(jnp.bfloat16), "seq", -1).astype(jnp.float32),
            shifted_2(d_values[:, :patch_rows].astype(jnp.bfloat16), "seq", -1).astype(jnp.float32),
        )
        d_packed = jnp.concatenate(
            (
                d_query.reshape(images, patch_rows, model_width),
                d_keys[:, patch_rows:] + back_keys,
                d_values[:, patch_rows:] + back_values,
            ),
            -1,
        ).astype(jnp.bfloat16)
        qkv_grad = outer_sum(normed, d_packed)
        d_normed = transposed(d_packed, qkv_weight[layer_index])
        unused_norm, norm_pull = jax.vjp(
            layer_norm,
            hidden,
            ln1_gain[layer_index].astype(jnp.float32),
            ln1_bias[layer_index].astype(jnp.float32),
        )
        d_input, ln1_gain_part, ln1_bias_part = norm_pull(d_normed)
        d_hidden = d_mid + d_input
        grads_qkv.insert(0, qkv_grad)
        grads_out.insert(0, out_grad)
        grads_up.insert(0, up_grad)
        grads_down.insert(0, down_grad)
        grads_g1.insert(0, ln1_gain_part)
        grads_b1.insert(0, ln1_bias_part)
        grads_g2.insert(0, ln2_gain_part)
        grads_b2.insert(0, ln2_bias_part)
        grads_ub.insert(0, up_bias_grad)
    d_embed_low = d_hidden.astype(jnp.bfloat16)
    patch_grad_part = outer_sum(latents.astype(jnp.bfloat16), d_embed_low)
    latents_grad = cot_latents * factor + transposed(d_embed_low, patch_weight)
    pos_part = jnp.sum(d_hidden, 0)
    class_part = jnp.sum(d_hidden, 1)
    logdet, class_sums = lax.psum((logdet_part, class_part), "seq")
    class_term = lax.dot_general(
        label_hot.astype(jnp.float32),
        class_sums,
        (((0,), (0,)), ((), ())),
        precision=precise,
        preferred_element_type=jnp.float32,
    )
    class_grad = lax.psum_scatter(class_term, "dp", scatter_dimension=0, tiled=True)
    pos_grad = lax.psum(pos_part, "dp")
    (
        patch_weight_grad,
        head_weight_grad,
        head_bias_grad,
        ln1_gain_grad,
        ln1_bias_grad,
        ln2_gain_grad,
        ln2_bias_grad,
        up_bias_grad,
    ) = lax.psum(
        (
            patch_grad_part,
            head_weight_grad,
            head_bias_grad,
            jnp.stack(grads_g1),
            jnp.stack(grads_b1),
            jnp.stack(grads_g2),
            jnp.stack(grads_b2),
            jnp.stack(grads_ub),
        ),
        ("dp", "seq"),
    )
    qkv_stack = jnp.stack(grads_qkv)
    out_stack = jnp.stack(grads_out)
    up_stack = jnp.stack(grads_up)
    down_stack = jnp.stack(grads_down)
    flat_parts = (
        lax.psum_scatter(eight_rows(qkv_stack), ("dp", "seq"), scatter_dimension=1, tiled=True),
        lax.psum_scatter(eight_rows(out_stack), ("dp", "seq"), scatter_dimension=1, tiled=True),
        lax.psum_scatter(eight_rows(up_stack), ("dp", "seq"), scatter_dimension=1, tiled=True),
        lax.psum_scatter(eight_rows(down_stack), ("dp", "seq"), scatter_dimension=1, tiled=True),
    )
    flat_qkv, flat_out, flat_up, flat_down = (
        lax.all_gather(
            flat_parts[0].astype(jnp.bfloat16), ("dp", "seq"), axis=1, tiled=True
        ).astype(jnp.float32),
        lax.all_gather(
            flat_parts[1].astype(jnp.bfloat16), ("dp", "seq"), axis=1, tiled=True
        ).astype(jnp.float32),
        lax.all_gather(
            flat_parts[2].astype(jnp.bfloat16), ("dp", "seq"), axis=1, tiled=True
        ).astype(jnp.float32),
        lax.all_gather(
            flat_parts[3].astype(jnp.bfloat16), ("dp", "seq"), axis=1, tiled=True
        ).astype(jnp.float32),
    )
    qkv_stack = flat_qkv.reshape(qkv_stack.shape)
    out_stack = flat_out.reshape(out_stack.shape)
    up_stack = flat_up.reshape(up_stack.shape)
    down_stack = flat_down.reshape(down_stack.shape)
    return (
        new_latents,
        logdet,
        latents_grad,
        patch_weight_grad,
        pos_grad,
        class_grad,
        ln1_gain_grad,
        ln1_bias_grad,
        qkv_stack,
        out_stack,
        ln2_gain_grad,
        ln2_bias_grad,
        up_stack,
        up_bias_grad,
        down_stack,
        head_weight_grad,
        head_bias_grad,
    )


def solution(mesh):
    in_specs = (
        P("dp", "seq", None),
        P("dp", "seq"),
        P(),
        P("dp"),
        P(),
        P("seq", None),
        P(),
        P(),
        P(),
        P(),
        P(),
        P(),
        P(),
        P(),
        P(),
        P(),
        P(),
        P(),
        P("dp", "seq", None),
        P("dp"),
    )
    out_specs = (
        P("dp", "seq", None),
        P("dp"),
        P("dp", "seq", None),
        P(),
        P("seq", None),
        P("dp", None),
        P(),
        P(),
        P(),
        P(),
        P(),
        P(),
        P(),
        P(),
        P(),
        P(),
        P(),
    )
    return jax.shard_map(local, mesh=mesh, in_specs=in_specs, out_specs=out_specs, check_vma=False)
```

profile of v0, /device:TPU:0, one launch (start us, length us, event | category | flops | bytes accessed | tf_op | source)
XLA Modules:
  0.0 1260.5 jit_solution(11902922079995836065)
XLA Ops:
  10.2 1.7 convolution_reduce_fusion
  14.1 3.0 collective-permute-start.2
  17.6 1.9 collective-permute-start.1
  19.5 2.0 collective-permute-start
  23.3 1.7 copy.52
  29.6 1.8 pad_maximum_fusion.2
  31.4 1.9 copy.53
  37.1 1.8 pad_maximum_fusion.1
  38.9 1.9 copy.51
  40.9 2.1 convolution_convert_fusion.3
  44.9 6.5 fusion.57
  57.1 2.0 multiply_subtract_fusion
  64.6 2.9 collective-permute-start.6
  68.8 1.7 copy.57
  70.5 4.3 collective-permute-start.5
  74.8 2.0 fusion.109
  76.8 1.8 pad_maximum_fusion.4
  78.6 1.9 copy.58
  80.6 1.6 fusion.136
  83.9 1.7 pad_maximum_fusion.3
  85.6 1.9 copy.56
  87.5 2.1 convolution_convert_fusion.2
  90.4 3.3 fusion.13
  93.8 5.5 convert_reduce_fusion
  99.3 2.3 multiply_reduce_fusion.1
  102.7 1.9 fusion.96
  104.6 3.5 reshape_stack.13
  108.2 2.6 fusion.60
  110.8 1.7 copy.59
  112.5 2.5 multiply_reduce_fusion
  120.2 1.6 collective-permute-done.8
  122.5 4.2 fusion.76
  126.7 7.2 reshape_stack.12
  134.6 6.5 fusion.125
  141.1 9.2 reshape_stack.14
  150.4 6.8 fusion.66
  157.2 9.3 reshape_stack.15
  166.6 42.8 %reduce-scatter.10.cloned.1.call-done = f32[8,2304]{1,0:T(8,128)} async-done(((f32[8,73728]{1,0:T(8,128)}), f32[8,2304]{1,0:T(8,128)}) %reduce-scatter.10.cloned.1.call-update) | async-done | bytes 73744 | tf_op jit(solution)/shard_map/reduce_scatter | solution.py:342
  211.0 123.2 %reduce-scatter.8.cloned.1.call-done = f32[8,6912]{1,0:T(8,128)} async-done(((f32[8,221184]{1,0:T(8,128)}), f32[8,6912]{1,0:T(8,128)}) %reduce-scatter.8.cloned.1.call-update) | async-done | bytes 221200 | tf_op jit(solution)/shard_map/reduce_scatter | solution.py:341
  334.2 1.6 convert_element_type.273
  335.8 139.6 %reduce-scatter.12.cloned.1.call-done = f32[8,9216]{1,0:T(8,128)} async-done(((f32[8,294912]{1,0:T(8,128)}), f32[8,9216]{1,0:T(8,128)}) %reduce-scatter.12.cloned.1.call-update) | async-done | bytes 294928 | tf_op jit(solution)/shard_map/reduce_scatter | solution.py:343
  475.4 1.6 convert_element_type.275
  477.1 139.7 %reduce-scatter.14.cloned.1.call-done = f32[8,9216]{1,0:T(8,128)} async-done(((f32[8,294912]{1,0:T(8,128)}), f32[8,9216]{1,0:T(8,128)}) %reduce-scatter.14.cloned.1.call-update) | async-done | bytes 294928 | tf_op jit(solution)/shard_map/reduce_scatter | solution.py:344
  616.8 1.6 convert_element_type.278
  618.5 1.9 fusion.108
  620.5 3.4 multiply_reduce_fusion.2
  624.9 1.8 convolution_bitcast_fusion
  626.8 1.9 fusion.65
  630.6 3.6 all-reduce.2
  634.2 1.9 broadcast_multiply_fusion
  639.2 41.3 %all-reduce = (f32[1,768]{1,0:T(1,128)}, f32[1,768]{1,0:T(1,128)}, f32[1,768]{1,0:T(1,128)}, f32[1,768]{1,0:T(1,128)}, f32[1,3072]{1,0:T(1,128)}, /*index=5*/f32[96]{0:T(128)}) all-reduce(f32[1,768]{1,0:T(1,128)S(1)} %stack.15, f32[1,768]{1,0:T(1,128)S(1)} %stack.16, ...), channel_id=1, replica_groups=mesh['dp'=16,'seq'=2] {'dp','seq'}, use_global_device_ids=true, to_apply=%region_26.27 | all-reduce | flops 6240 | bytes 49920 | tf_op jit(solution)/shard_map/psum | solution.py:323
  680.5 3.1 reshape.960
  683.6 51.8 %all-gather.5.cloned.1.call-done = bf16[8,221184]{1,0:T(8,128)(2,1)} async-done(((bf16[8,6912]{1,0:T(8,128)(2,1)}), bf16[8,221184]{1,0:T(8,128)(2,1)}) %all-gather.5.cloned.1.call-update) | async-done | bytes 3538960 | tf_op jit(solution)/shard_map/all_gather | solution.py:347
  735.4 6.3 reshape.958
  741.8 59.6 %all-gather.9.cloned.1.call-done = bf16[8,294912]{1,0:T(8,128)(2,1)} async-done(((bf16[8,9216]{1,0:T(8,128)(2,1)}), bf16[8,294912]{1,0:T(8,128)(2,1)}) %all-gather.9.cloned.1.call-update) | async-done | bytes 4718608 | tf_op jit(solution)/shard_map/all_gather | solution.py:353
  801.4 7.9 reshape.962
  809.3 57.4 %all-gather.11.cloned.1.call-done = bf16[8,294912]{1,0:T(8,128)(2,1)} async-done(((bf16[8,9216]{1,0:T(8,128)(2,1)}), bf16[8,294912]{1,0:T(8,128)(2,1)}) %all-gather.11.cloned.1.call-update) | async-done | bytes 4718608 | tf_op jit(solution)/shard_map/all_gather | solution.py:356
  866.7 7.9 reshape.964
  874.6 123.7 %all-reduce.8.cloned.1.call-done = (f32[48,768]{1,0:T(8,128)}, f32[768,96]{0,1:T(8,128)}) async-done(((f32[48,768]{1,0:T(8,128)}, f32[768,96]{0,1:T(8,128)}), (f32[48,768]{1,0:T(8,128)}, f32[768,96]{0,1:T(8,128)})) %all-reduce.8.cloned.1.call-update) | async-done | bytes 442384 | tf_op jit(solution)/shard_map/psum | solution.py:323
  998.3 115.3 %all-reduce.6.cloned.1.call-done = f32[128,768]{1,0:T(8,128)} async-done(((f32[128,768]{1,0:T(8,128)}), f32[128,768]{1,0:T(8,128)}) %all-reduce.6.cloned.1.call-update) | async-done | bytes 393232 | tf_op jit(solution)/shard_map/psum | solution.py:313
  1113.7 135.2 %reduce-scatter.6.cloned.1.call-done = f32[64,768]{1,0:T(8,128)} async-done(((f32[1024,768]{1,0:T(8,128)}), f32[64,768]{1,0:T(8,128)}) %reduce-scatter.6.cloned.1.call-update) | async-done | bytes 196624 | tf_op jit(solution)/shard_map/reduce_scatter | solution.py:312
  1248.9 1.6 copy.66
  1250.5 1.8 copy.67
  1252.3 1.7 copy.68
  (220 shorter events, 45.8 us)
Async XLA Ops:
  7.2 5.4 copy-start
  7.2 5.3 copy-start.51
  7.2 5.3 copy-start.50
  7.2 202.2 %reduce-scatter.10.cloned.1.call-start = ((), (), s32[]{:S(2)}) async-start(), calls=%async_computation.9 | async-start | bytes 2433024 | tf_op jit(solution)/shard_map/reduce_scatter | solution.py:342
  7.3 4.6 copy-start.23
  7.3 4.6 copy-start.27
  7.3 4.6 copy-start.29
  12.5 50.5 %copy-start.32 = (f32[768]{0:T(1024)}, f32[768]{0:T(1024)S(1)}, u32[]{:S(2)}) copy-start(f32[768]{0:T(1024)S(1)} %get-tuple-element.71) | copy-start | bytes 9220
  12.6 4.6 copy-start.55
  14.1 15.5 %collective-permute-start.2 = (bf16[1,128,768]{2,1,0:T(8,128)(2,1)}, bf16[1,128,768]{2,1,0:T(8,128)(2,1)}, u32[]{:S(2)}, u32[]{:S(2)}) collective-permute-start(bf16[1,128,768]{2,1,0:T(8,128)(2,1)} %get-tuple-element.46), channel_id=1, source_target_pairs={{0,1},{2,3},{4,5},{6,7},{8,9},{10,11},{12,13},{14,15},{16,17},{18,... | collective-permute-start | bytes 589832 | tf_op jit(solution)/shard_map/ppermute | solution.py:14
  17.6 9.9 collective-permute-start.1
  19.5 17.6 %collective-permute-start = (bf16[1,128,768]{2,1,0:T(8,128)(2,1)}, bf16[1,128,768]{2,1,0:T(8,128)(2,1)}, u32[]{:S(2)}, u32[]{:S(2)}) collective-permute-start(bf16[1,128,768]{2,1,0:T(8,128)(2,1)} %get-tuple-element.48), channel_id=1, source_target_pairs={{0,1},{2,3},{4,5},{6,7},{8,9},{10,11},{12,13},{14,15},{16,17},{18,... | collective-permute-start | bytes 589832 | tf_op jit(solution)/shard_map/ppermute | solution.py:14
  23.3 21.6 %copy-start.34 = (f32[768]{0:T(1024)}, f32[768]{0:T(1024)S(1)}, u32[]{:S(2)}) copy-start(f32[768]{0:T(1024)S(1)} %get-tuple-element.73) | copy-start | bytes 9220
  34.9 1.1 copy-start.8
  40.8 2.1 copy-start.9
  40.9 2.1 copy-start.13
  53.3 2.1 collective-permute-start.3
  57.1 2.0 copy-start.31
  59.7 2.8 copy-start.30
  62.3 1.5 copy-start.3
  62.4 1.4 copy-start.43
  64.6 12.2 collective-permute-start.6
  67.5 7.3 collective-permute-start.4
  70.5 13.3 %collective-permute-start.5 = (bf16[1,128,768]{2,1,0:T(8,128)(2,1)}, bf16[1,128,768]{2,1,0:T(8,128)(2,1)}, u32[]{:S(2)}, u32[]{:S(2)}) collective-permute-start(bf16[1,128,768]{2,1,0:T(8,128)(2,1)} %get-tuple-element.45), channel_id=1, source_target_pairs={{0,1},{2,3},{4,5},{6,7},{8,9},{10,11},{12,13},{14,15},{16,17},{18,... | collective-permute-start | bytes 589832 | tf_op jit(solution)/shard_map/ppermute | solution.py:14
  80.6 3.3 copy-start.22
  82.2 1.1 copy-start.1
  87.5 2.2 copy-start.4
  87.5 2.2 copy-start.10
  90.1 11.5 copy-start.7
  90.1 11.5 copy-start.39
  90.4 11.3 copy-start.46
  90.4 3.4 copy-start.17
  90.4 8.9 slice-start
  93.8 5.5 copy-start.11
  93.8 5.5 slice-start.1
  99.3 2.3 copy-start.18
  108.1 226.0 %reduce-scatter.8.cloned.1.call-start = ((), (), s32[]{:S(2)}) async-start(), calls=%async_computation.7 | async-start | bytes 7299072 | tf_op jit(solution)/shard_map/reduce_scatter | solution.py:341
  112.5 2.5 copy-start.2
  116.0 1.8 copy-start.19
  116.3 3.4 copy-start.16
  116.3 3.9 collective-permute-start.7
  118.3 4.3 copy-start.5
  118.3 4.3 copy-start.33
  118.3 4.2 copy-start.44
  118.3 4.2 copy-start.48
  118.3 3.5 collective-permute-start.8
  120.1 1.7 copy-start.26
  120.2 1.6 copy-start.24
  133.9 341.5 %reduce-scatter.12.cloned.1.call-start = ((), (), s32[]{:S(2)}) async-start(), calls=%async_computation.11 | async-start | bytes 9732096 | tf_op jit(solution)/shard_map/reduce_scatter | solution.py:343
  150.4 466.4 %reduce-scatter.14.cloned.1.call-start = ((), (), s32[]{:S(2)}) async-start(), calls=%async_computation.13 | async-start | bytes 9732096 | tf_op jit(solution)/shard_map/reduce_scatter | solution.py:344
  166.5 453.9 %copy-start.45 = (f32[128]{0:T(128)S(1)}, f32[128]{0:T(128)}, u32[]{:S(2)}) copy-start(f32[128]{0:T(128)} %copy-done.43) | copy-start | bytes 1540
  166.5 453.9 %copy-start.49 = (f32[128]{0:T(128)S(1)}, f32[128]{0:T(128)}, u32[]{:S(2)}) copy-start(f32[128]{0:T(128)} %copy-done.47) | copy-start | bytes 1540
  166.6 513.9 %all-gather.7.cloned.1.call-start = ((), (), s32[]{:S(2)}) async-start(), calls=%async_computation.10 | async-start | bytes 1216512 | tf_op jit(solution)/shard_map/all_gather | solution.py:350
  210.9 524.5 %all-gather.5.cloned.1.call-start = ((), (), s32[]{:S(2)}) async-start(), calls=%async_computation.8 | async-start | bytes 3649536 | tf_op jit(solution)/shard_map/all_gather | solution.py:347
  335.8 465.6 %all-gather.9.cloned.1.call-start = ((), (), s32[]{:S(2)}) async-start(), calls=%async_computation.12 | async-start | bytes 4866048 | tf_op jit(solution)/shard_map/all_gather | solution.py:353
  477.1 389.6 %all-gather.11.cloned.1.call-start = ((), (), s32[]{:S(2)}) async-start(), calls=%async_computation.14 | async-start | bytes 4866048 | tf_op jit(solution)/shard_map/all_gather | solution.py:356
  618.5 379.9 %all-reduce.8.cloned.1.call-start = ((), (), s32[]{:S(2)}) async-start(), calls=%async_computation.15 | async-start | bytes 884736 | tf_op jit(solution)/shard_map/psum | solution.py:323
  620.4 3.4 copy-start.53
  620.4 3.4 copy-start.6
  620.4 3.6 copy-start.15
  628.7 485.0 %all-reduce.6.cloned.1.call-start = ((), (), s32[]{:S(2)}) async-start(), calls=%async_computation.5 | async-start | bytes 786432 | tf_op jit(solution)/shard_map/psum | solution.py:313
  629.2 619.7 %reduce-scatter.6.cloned.1.call-start = ((), (), s32[]{:S(2)}) async-start(), calls=%async_computation.6 | async-start | bytes 3342336 | tf_op jit(solution)/shard_map/reduce_scatter | solution.py:312
  636.2 2.3 copy-start.42
  636.2 2.3 copy-start.41
  (14 other events, 10.3 us)
Sparse Core Ops, SparseCore 0:
  108.3 101.0 reduce-scatter.9
  216.0 118.1 reduce-scatter.7
  340.6 134.7 reduce-scatter.11
  482.2 134.5 reduce-scatter.13
  619.6 53.5 all-gather.6
  676.5 58.9 all-gather.4
  738.9 62.4 all-gather.8
  804.3 62.4 all-gather.10
  873.2 125.0 all-reduce.7
  1004.8 108.8 all-reduce.5
  1119.2 129.6 reduce-scatter.5
where the time goes:
time: 1260 us
  waiting for transfers between devices  991 us (79%)
  local copies, waits for them, and re-layouts  84.4 us (7%)
  matrix products  68.3 us (5%)
  blocking collectives  44.9 us (4%)
  other arithmetic  34.9 us (3%)
  starting transfers between devices  20.1 us (2%)
  between operations  17 us (1%)
    reduce_scatter x1, waiting for transfers between devices, local(): lax.psum_scatter(eight_rows(down_stack), ('dp', 'seq'), scatter_dimension...  140 us
    reduce_scatter x1, waiting for transfers between devices, local(): lax.psum_scatter(eight_rows(up_stack), ('dp', 'seq'), scatter_dimension=1...  140 us
    reduce_scatter x1, waiting for transfers between devices, local(): lax.psum_scatter(class_term, 'dp', scatter_dimension=0, tiled=True)  135 us
    psum x1, waiting for transfers between devices, local(): lax.psum((patch_grad_part, head_weight_grad, head_bias_grad, jnp.stack(gr...  124 us
    reduce_scatter x1, waiting for transfers between devices, local(): lax.psum_scatter(eight_rows(qkv_stack), ('dp', 'seq'), scatter_dimension=...  123 us
    psum x1, waiting for transfers between devices, local(): pos_grad = lax.psum(pos_part, 'dp')  115 us
    all_gather x1, waiting for transfers between devices, local(): lax.all_gather(flat_parts[2].astype(jnp.bfloat16), ('dp', 'seq'), axis=1,...  59.6 us
    all_gather x1, waiting for transfers between devices, local(): lax.all_gather(flat_parts[3].astype(jnp.bfloat16), ('dp', 'seq'), axis=1,...  57.4 us
  transfers between devices with their start and end apart: 20, of which 12 were waited for; matrix products, arithmetic and copies ran while one was open for 10% of the time, Pallas kernels for 0%

commit v1 on v0

--- a/solution.py
+++ b/solution.py
@@ -6,6 +6,15 @@
 HEAD_DIM = 64
 precise = lax.Precision.HIGHEST
 norm_eps = 1e-05
+
+
+def added_up(shard, axis):
+    devices = lax.axis_size(axis)
+    result, far = (shard, 1)
+    while far < devices:
+        result = result + lax.ppermute(result, axis, [(i, i ^ far) for i in range(devices)])
+        far = 2 * far
+    return result
 
 
 def shifted_2(shard, axis, by):
@@ -310,7 +319,7 @@
         preferred_element_type=jnp.float32,
     )
     class_grad = lax.psum_scatter(class_term, "dp", scatter_dimension=0, tiled=True)
-    pos_grad = lax.psum(pos_part, "dp")
+    pos_grad = added_up(pos_part, "dp")
     (
         patch_weight_grad,
         head_weight_grad,

time: 1260 us -> 1030 us (0.82)
  waiting for transfers between devices: 991 us -> 739 us
    reduce_scatter x1, waiting for transfers between devices: 135 us -> 0.01 us  [local(): lax.psum_scatter(class_term, 'dp', scatter_dimension=0, tiled=True)]
    psum x1 -> x0, waiting for transfers between devices: 115 us -> none  [local(): pos_grad = lax.psum(pos_part, 'dp')]
    all_gather x1, waiting for transfers between devices: 51.8 us -> 9.61 us  [local(): lax.all_gather(flat_parts[0].astype(jnp.bfloat16), ('dp', 'seq'), axis=1,...]
    ppermute x0 -> x4, waiting for transfers between devices: none -> 36.2 us  [added_up(): lax.ppermute(result, axis, [(i, i ^ far) for i in range(devices)])]
  transfers between devices with their start and end apart: 20 -> 23, of which waited for: 12 -> 13; matrix products, arithmetic and copies ran while one was open for 10% -> 12% of each run, Pallas kernels for 0% -> 0%
where the time goes in v1:
time: 1030 us; the launch traced here: 1020 us
  waiting for transfers between devices  739 us (72%)
  local copies, waits for them, and re-layouts  81.1 us (8%)
  matrix products  68.3 us (7%)
  blocking collectives  47.3 us (5%)
  other arithmetic  38.7 us (4%)
  starting transfers between devices  28.3 us (3%)
  between operations  18.7 us (2%)
    reduce_scatter x1, waiting for transfers between devices, local(): lax.psum_scatter(eight_rows(down_stack), ('dp', 'seq'), scatter_dimension...  140 us
    reduce_scatter x1, waiting for transfers between devices, local(): lax.psum_scatter(eight_rows(up_stack), ('dp', 'seq'), scatter_dimension=1...  140 us
    psum x1, waiting for transfers between devices, local(): lax.psum((patch_grad_part, head_weight_grad, head_bias_grad, jnp.stack(gr...  124 us
    reduce_scatter x1, waiting for transfers between devices, local(): lax.psum_scatter(eight_rows(qkv_stack), ('dp', 'seq'), scatter_dimension=...  123 us
    all_gather x1, waiting for transfers between devices, local(): lax.all_gather(flat_parts[2].astype(jnp.bfloat16), ('dp', 'seq'), axis=1,...  64.7 us
    all_gather x1, waiting for transfers between devices, local(): lax.all_gather(flat_parts[3].astype(jnp.bfloat16), ('dp', 'seq'), axis=1,...  57.5 us
    psum x1, blocking collectives, local(): lax.psum((patch_grad_part, head_weight_grad, head_bias_grad, jnp.stack(gr...  43.6 us
    reduce_scatter x1, waiting for transfers between devices, local(): lax.psum_scatter(eight_rows(out_stack), ('dp', 'seq'), scatter_dimension=...  42.8 us
  transfers between devices with their start and end apart: 23, of which 13 were waited for; matrix products, arithmetic and copies ran while one was open for 12% of the time, Pallas kernels for 0%

profile of v1, /device:TPU:0, one launch (start us, length us, event | category | flops | bytes accessed | tf_op | source)
XLA Modules:
  0.0 1021.4 jit_solution(17994506605280541815)
XLA Ops:
  11.0 1.7 convolution_reduce_fusion
  14.9 3.0 collective-permute-start.2
  18.5 1.8 collective-permute-start.1
  20.3 2.0 collective-permute-start
  24.1 1.7 copy.52
  30.4 1.8 pad_maximum_fusion.2
  32.2 1.9 copy.53
  37.9 1.8 pad_maximum_fusion.1
  39.7 1.9 copy.51
  41.6 2.1 convolution_convert_fusion.3
  45.6 6.5 fusion.57
  57.9 2.0 multiply_subtract_fusion
  65.4 2.9 collective-permute-start.6
  69.6 1.7 copy.57
  71.3 4.5 collective-permute-start.5
  75.9 2.0 fusion.109
  77.9 1.8 pad_maximum_fusion.4
  79.7 1.9 copy.58
  81.6 1.6 fusion.136
  84.9 1.7 pad_maximum_fusion.3
  86.6 1.9 copy.56
  88.5 2.1 convolution_convert_fusion.2
  91.4 3.3 fusion.13
  94.8 5.5 convert_reduce_fusion
  100.3 2.3 multiply_reduce_fusion.1
  103.8 1.9 fusion.96
  105.6 3.5 reshape_stack.13
  109.2 2.6 fusion.60
  111.8 1.7 copy.59
  113.6 2.5 multiply_reduce_fusion
  123.6 4.2 fusion.76
  127.7 7.2 reshape_stack.12
  135.6 6.5 fusion.125
  142.2 9.2 reshape_stack.14
  151.4 6.8 fusion.66
  158.2 9.3 reshape_stack.15
  167.6 42.8 %reduce-scatter.10.cloned.1.call-done = f32[8,2304]{1,0:T(8,128)} async-done(((f32[8,73728]{1,0:T(8,128)}), f32[8,2304]{1,0:T(8,128)}) %reduce-scatter.10.cloned.1.call-update) | async-done | bytes 73744 | tf_op jit(solution)/shard_map/reduce_scatter | solution.py:351
  212.0 123.3 %reduce-scatter.8.cloned.1.call-done = f32[8,6912]{1,0:T(8,128)} async-done(((f32[8,221184]{1,0:T(8,128)}), f32[8,6912]{1,0:T(8,128)}) %reduce-scatter.8.cloned.1.call-update) | async-done | bytes 221200 | tf_op jit(solution)/shard_map/reduce_scatter | solution.py:350
  335.2 1.6 convert_element_type.273
  336.9 139.6 %reduce-scatter.12.cloned.1.call-done = f32[8,9216]{1,0:T(8,128)} async-done(((f32[8,294912]{1,0:T(8,128)}), f32[8,9216]{1,0:T(8,128)}) %reduce-scatter.12.cloned.1.call-update) | async-done | bytes 294928 | tf_op jit(solution)/shard_map/reduce_scatter | solution.py:352
  476.5 1.6 convert_element_type.275
  478.2 139.8 %reduce-scatter.14.cloned.1.call-done = f32[8,9216]{1,0:T(8,128)} async-done(((f32[8,294912]{1,0:T(8,128)}), f32[8,9216]{1,0:T(8,128)}) %reduce-scatter.14.cloned.1.call-update) | async-done | bytes 294928 | tf_op jit(solution)/shard_map/reduce_scatter | solution.py:353
  618.0 1.6 convert_element_type.278
  621.0 1.9 fusion.108
  623.0 3.4 multiply_reduce_fusion.2
  627.5 3.6 all-reduce.2
  631.1 1.8 convolution_bitcast_fusion
  633.0 1.9 broadcast_multiply_fusion
  636.5 10.3 %collective-permute-done.9 = f32[128,768]{1,0:T(8,128)S(1)} collective-permute-done((f32[128,768]{1,0:T(8,128)}, f32[128,768]{1,0:T(8,128)S(1)}, u32[]{:S(2)}, u32[]{:S(2)}) %collective-permute-start.9) | collective-permute-done | bytes 393248 | tf_op jit(solution)/shard_map/ppermute | solution.py:15
  649.0 9.2 collective-permute-done.10
  659.9 16.7 %collective-permute-done.11 = f32[128,768]{1,0:T(8,128)S(1)} collective-permute-done((f32[128,768]{1,0:T(8,128)S(1)}, f32[128,768]{1,0:T(8,128)S(1)}, u32[]{:S(2)}, u32[]{:S(2)}) %collective-permute-start.11) | collective-permute-done | bytes 393248 | tf_op jit(solution)/shard_map/ppermute | solution.py:15
  677.3 3.6 collective-permute-start.12
  682.5 43.6 %all-reduce = (f32[1,768]{1,0:T(1,128)}, f32[1,768]{1,0:T(1,128)}, f32[1,768]{1,0:T(1,128)}, f32[1,768]{1,0:T(1,128)}, f32[1,3072]{1,0:T(1,128)}, /*index=5*/f32[96]{0:T(128)}) all-reduce(f32[1,768]{1,0:T(1,128)S(1)} %stack.15, f32[1,768]{1,0:T(1,128)S(1)} %stack.16, ...), channel_id=1, replica_groups=mesh['dp'=16,'seq'=2] {'dp','seq'}, use_global_device_ids=true, to_apply=%region_25.26 | all-reduce | flops 6240 | bytes 49920 | tf_op jit(solution)/shard_map/psum | solution.py:332
  726.2 1.9 fusion.65
  728.0 1.9 add.296
  729.9 3.1 reshape.960
  733.1 9.6 all-gather.5.cloned.1.call-done
  742.7 6.3 reshape.958
  749.0 64.7 %all-gather.9.cloned.1.call-done = bf16[8,294912]{1,0:T(8,128)(2,1)} async-done(((bf16[8,9216]{1,0:T(8,128)(2,1)}), bf16[8,294912]{1,0:T(8,128)(2,1)}) %all-gather.9.cloned.1.call-update) | async-done | bytes 4718608 | tf_op jit(solution)/shard_map/all_gather | solution.py:362
  813.8 7.9 reshape.962
  821.7 57.5 %all-gather.11.cloned.1.call-done = bf16[8,294912]{1,0:T(8,128)(2,1)} async-done(((bf16[8,9216]{1,0:T(8,128)(2,1)}), bf16[8,294912]{1,0:T(8,128)(2,1)}) %all-gather.11.cloned.1.call-update) | async-done | bytes 4718608 | tf_op jit(solution)/shard_map/all_gather | solution.py:365
  879.1 7.9 reshape.964
  887.0 123.7 %all-reduce.5.cloned.1.call-done = (f32[48,768]{1,0:T(8,128)}, f32[768,96]{0,1:T(8,128)}) async-done(((f32[48,768]{1,0:T(8,128)}, f32[768,96]{0,1:T(8,128)}), (f32[48,768]{1,0:T(8,128)}, f32[768,96]{0,1:T(8,128)})) %all-reduce.5.cloned.1.call-update) | async-done | bytes 442384 | tf_op jit(solution)/shard_map/psum | solution.py:332
  1012.4 1.7 copy.66
  (234 shorter events, 53.0 us)
Async XLA Ops:
  8.0 5.4 copy-start
  8.0 5.3 copy-start.54
  8.0 5.3 copy-start.53
  8.1 202.4 %reduce-scatter.10.cloned.1.call-start = ((), (), s32[]{:S(2)}) async-start(), calls=%async_computation.8 | async-start | bytes 2433024 | tf_op jit(solution)/shard_map/reduce_scatter | solution.py:351
  8.1 4.6 copy-start.23
  8.1 4.6 copy-start.27
  8.1 4.6 copy-start.29
  13.4 50.5 %copy-start.33 = (f32[768]{0:T(1024)}, f32[768]{0:T(1024)S(1)}, u32[]{:S(2)}) copy-start(f32[768]{0:T(1024)S(1)} %get-tuple-element.71) | copy-start | bytes 9220
  13.4 4.6 copy-start.58
  14.9 15.5 %collective-permute-start.2 = (bf16[1,128,768]{2,1,0:T(8,128)(2,1)}, bf16[1,128,768]{2,1,0:T(8,128)(2,1)}, u32[]{:S(2)}, u32[]{:S(2)}) collective-permute-start(bf16[1,128,768]{2,1,0:T(8,128)(2,1)} %get-tuple-element.46), channel_id=1, source_target_pairs={{0,1},{2,3},{4,5},{6,7},{8,9},{10,11},{12,13},{14,15},{16,17},{18,... | collective-permute-start | bytes 589832 | tf_op jit(solution)/shard_map/ppermute | solution.py:23
  18.5 9.8 collective-permute-start.1
  20.3 17.6 %collective-permute-start = (bf16[1,128,768]{2,1,0:T(8,128)(2,1)}, bf16[1,128,768]{2,1,0:T(8,128)(2,1)}, u32[]{:S(2)}, u32[]{:S(2)}) collective-permute-start(bf16[1,128,768]{2,1,0:T(8,128)(2,1)} %get-tuple-element.48), channel_id=1, source_target_pairs={{0,1},{2,3},{4,5},{6,7},{8,9},{10,11},{12,13},{14,15},{16,17},{18,... | collective-permute-start | bytes 589832 | tf_op jit(solution)/shard_map/ppermute | solution.py:23
  24.1 21.6 %copy-start.35 = (f32[768]{0:T(1024)}, f32[768]{0:T(1024)S(1)}, u32[]{:S(2)}) copy-start(f32[768]{0:T(1024)S(1)} %get-tuple-element.73) | copy-start | bytes 9220
  41.6 2.1 copy-start.9
  41.6 2.1 copy-start.13
  54.1 2.1 collective-permute-start.3
  57.8 2.0 copy-start.32
  60.5 2.8 copy-start.30
  65.4 12.4 %collective-permute-start.6 = (bf16[1,128,768]{2,1,0:T(8,128)(2,1)}, bf16[1,128,768]{2,1,0:T(8,128)(2,1)}, u32[]{:S(2)}, u32[]{:S(2)}) collective-permute-start(bf16[1,128,768]{2,1,0:T(8,128)(2,1)} %get-tuple-element.43), channel_id=1, source_target_pairs={{0,1},{2,3},{4,5},{6,7},{8,9},{10,11},{12,13},{14,15},{16,17},{18,... | collective-permute-start | bytes 589832 | tf_op jit(solution)/shard_map/ppermute | solution.py:23
  68.3 7.5 collective-permute-start.4
  71.3 13.6 %collective-permute-start.5 = (bf16[1,128,768]{2,1,0:T(8,128)(2,1)}, bf16[1,128,768]{2,1,0:T(8,128)(2,1)}, u32[]{:S(2)}, u32[]{:S(2)}) collective-permute-start(bf16[1,128,768]{2,1,0:T(8,128)(2,1)} %get-tuple-element.45), channel_id=1, source_target_pairs={{0,1},{2,3},{4,5},{6,7},{8,9},{10,11},{12,13},{14,15},{16,17},{18,... | collective-permute-start | bytes 589832 | tf_op jit(solution)/shard_map/ppermute | solution.py:23
  81.6 3.3 copy-start.22
  88.5 2.2 copy-start.4
  88.5 2.2 copy-start.10
  91.1 11.5 %copy-start.7 = (f32[128,768]{1,0:T(8,128)}, f32[128,768]{1,0:T(8,128)S(1)}, u32[]{:S(2)}) copy-start(f32[128,768]{1,0:T(8,128)S(1)} %get-tuple-element.64) | copy-start | bytes 1179652
  91.2 11.5 %copy-start.40 = (f32[128]{0:T(128)}, f32[128]{0:T(128)S(1)}, u32[]{:S(2)}) copy-start(f32[128]{0:T(128)S(1)} %broadcast_multiply_fusion.1) | copy-start | bytes 1540
  91.4 11.3 %copy-start.47 = (f32[128]{0:T(128)}, f32[128]{0:T(128)S(1)}, u32[]{:S(2)}) copy-start(f32[128]{0:T(128)S(1)} %fusion.112) | copy-start | bytes 1540
  91.4 3.4 copy-start.17
  91.4 8.9 slice-start
  94.8 5.5 copy-start.11
  94.8 5.5 slice-start.1
  100.3 2.3 copy-start.18
  109.2 226.1 %reduce-scatter.8.cloned.1.call-start = ((), (), s32[]{:S(2)}) async-start(), calls=%async_computation.6 | async-start | bytes 7299072 | tf_op jit(solution)/shard_map/reduce_scatter | solution.py:350
  113.6 2.5 copy-start.2
  117.0 1.7 copy-start.19
  117.3 3.4 copy-start.16
  117.3 3.9 collective-permute-start.7
  119.3 4.3 copy-start.5
  119.3 4.3 copy-start.34
  119.3 4.2 copy-start.45
  119.3 4.2 copy-start.49
  119.3 3.5 collective-permute-start.8
  135.0 341.5 %reduce-scatter.12.cloned.1.call-start = ((), (), s32[]{:S(2)}) async-start(), calls=%async_computation.10 | async-start | bytes 9732096 | tf_op jit(solution)/shard_map/reduce_scatter | solution.py:352
  151.4 466.6 %reduce-scatter.14.cloned.1.call-start = ((), (), s32[]{:S(2)}) async-start(), calls=%async_computation.12 | async-start | bytes 9732096 | tf_op jit(solution)/shard_map/reduce_scatter | solution.py:353
  167.6 455.4 %copy-start.46 = (f32[128]{0:T(128)S(1)}, f32[128]{0:T(128)}, u32[]{:S(2)}) copy-start(f32[128]{0:T(128)} %copy-done.44) | copy-start | bytes 1540
  167.6 455.4 %copy-start.50 = (f32[128]{0:T(128)S(1)}, f32[128]{0:T(128)}, u32[]{:S(2)}) copy-start(f32[128]{0:T(128)} %copy-done.48) | copy-start | bytes 1540
  167.6 562.3 %all-gather.7.cloned.1.call-start = ((), (), s32[]{:S(2)}) async-start(), calls=%async_computation.9 | async-start | bytes 1216512 | tf_op jit(solution)/shard_map/all_gather | solution.py:359
  211.9 530.7 %all-gather.5.cloned.1.call-start = ((), (), s32[]{:S(2)}) async-start(), calls=%async_computation.7 | async-start | bytes 3649536 | tf_op jit(solution)/shard_map/all_gather | solution.py:356
  336.9 476.9 %all-gather.9.cloned.1.call-start = ((), (), s32[]{:S(2)}) async-start(), calls=%async_computation.11 | async-start | bytes 4866048 | tf_op jit(solution)/shard_map/all_gather | solution.py:362
  478.2 401.0 %all-gather.11.cloned.1.call-start = ((), (), s32[]{:S(2)}) async-start(), calls=%async_computation.13 | async-start | bytes 4866048 | tf_op jit(solution)/shard_map/all_gather | solution.py:365
  619.7 391.1 %all-reduce.5.cloned.1.call-start = ((), (), s32[]{:S(2)}) async-start(), calls=%async_computation.14 | async-start | bytes 884736 | tf_op jit(solution)/shard_map/psum | solution.py:332
  623.0 3.4 copy-start.56
  623.0 3.4 copy-start.6
  623.0 3.6 copy-start.15
  633.0 377.8 %reduce-scatter.6.cloned.1.call-start = ((), (), s32[]{:S(2)}) async-start(), calls=%async_computation.5 | async-start | bytes 3342336 | tf_op jit(solution)/shard_map/reduce_scatter | solution.py:321
  635.0 46.0 %copy-start.31 = (bf16[1,128,96]{1,2,0:T(8,128)(2,1)S(1)}, bf16[1,128,96]{1,2,0:T(8,128)(2,1)}, u32[]{:S(2)}) copy-start(bf16[1,128,96]{1,2,0:T(8,128)(2,1)} %copy-done.30) | copy-start | bytes 73732
  635.0 47.5 %copy-start.43 = (f32[768]{0:T(1024)S(1)}, f32[768]{0:T(1024)}, u32[]{:S(2)}) copy-start(f32[768]{0:T(1024)} %get-tuple-element.19) | copy-start | bytes 9220
  635.0 47.5 %copy-start.42 = (f32[768]{0:T(1024)S(1)}, f32[768]{0:T(1024)}, u32[]{:S(2)}) copy-start(f32[768]{0:T(1024)} %get-tuple-element.23) | copy-start | bytes 9220
  635.0 47.5 %copy-start.52 = (f32[768]{0:T(1024)S(1)}, f32[768]{0:T(1024)}, u32[]{:S(2)}) copy-start(f32[768]{0:T(1024)} %get-tuple-element.21) | copy-start | bytes 9220
  635.0 47.5 %copy-start.51 = (f32[768]{0:T(1024)S(1)}, f32[768]{0:T(1024)}, u32[]{:S(2)}) copy-start(f32[768]{0:T(1024)} %get-tuple-element.24) | copy-start | bytes 9220
  635.0 11.8 %collective-permute-start.9 = (f32[128,768]{1,0:T(8,128)}, f32[128,768]{1,0:T(8,128)S(1)}, u32[]{:S(2)}, u32[]{:S(2)}) collective-permute-start(f32[128,768]{1,0:T(8,128)} %get-tuple-element.36), channel_id=1, source_target_pairs={{0,2},{2,0},{4,6},{6,4},{8,10},{10,8},{12,14},{14,12},{16,18},{18,... | collective-permute-start | bytes 1179656 | tf_op jit(solution)/shard_map/ppermute | solution.py:15
  647.9 10.4 %collective-permute-start.10 = (f32[128,768]{1,0:T(8,128)S(1)}, f32[128,768]{1,0:T(8,128)S(1)}, u32[]{:S(2)}, u32[]{:S(2)}) collective-permute-start(f32[128,768]{1,0:T(8,128)S(1)} %add.293), channel_id=1, source_target_pairs={{0,4},{2,6},{4,0},{6,2},{8,12},{10,14},{12,8},{14,10},{16,20},{18,... | collective-permute-start | bytes 1179656 | tf_op jit(solution)/shard_map/ppermute | solution.py:15
  658.3 18.2 %collective-permute-start.11 = (f32[128,768]{1,0:T(8,128)S(1)}, f32[128,768]{1,0:T(8,128)S(1)}, u32[]{:S(2)}, u32[]{:S(2)}) collective-permute-start(f32[128,768]{1,0:T(8,128)S(1)} %add.294), channel_id=1, source_target_pairs={{0,8},{2,10},{4,12},{6,14},{8,0},{10,2},{12,4},{14,6},{16,24},{18,... | collective-permute-start | bytes 1179656 | tf_op jit(solution)/shard_map/ppermute | solution.py:15
  677.3 50.7 %collective-permute-start.12 = (f32[128,768]{1,0:T(8,128)}, f32[128,768]{1,0:T(8,128)}, u32[]{:S(2)}, u32[]{:S(2)}) collective-permute-start(f32[128,768]{1,0:T(8,128)} %add.295), channel_id=1, source_target_pairs={{0,16},{2,18},{4,20},{6,22},{8,24},{10,26},{12,28},{14,30},{16,0},... | collective-permute-start | bytes 1179656 | tf_op jit(solution)/shard_map/ppermute | solution.py:15
  (20 other events, 18.9 us)
Sparse Core Ops, SparseCore 0:
  109.3 101.0 reduce-scatter.9
  217.0 118.1 reduce-scatter.7
  341.7 134.7 reduce-scatter.11
  483.3 134.7 reduce-scatter.13
  620.8 56.8 all-gather.6
  681.0 61.6 all-gather.4
  746.2 67.5 all-gather.8
  816.6 62.4 all-gather.10
  885.7 125.0 all-reduce.4
Sparse Core Ops, SparseCore 1:
  639.8 148.1 reduce-scatter.5
